TPU v7x, 256 devices: a whole 4x4x8 slice. The times are simulated.
256 devices in a mesh: row: 8 (over y, core), col: 32 (over z, x).
Axes of the slice: x: 4, y: 4, z: 8, core: 2. Of those that a mesh axis runs over, the one named last changes fastest.
Arguments:
- diag_block: float32 [1024, 1024], P('row')
- panel: bfloat16 [64, 1024, 1024], P('col', 'row'), may hold values from -1 to 1
- trailing: bfloat16 [32, 12, 1024, 1024], P('col', None, 'row'), may hold values from -6 to 6
- slot_rows: int32 [32, 12], replicated, may hold values from -1 to 63, as said below
- slot_cols: int32 [32, 12], replicated, may hold values from 0 to 1, as said below
Outputs:
- panel_factor: bfloat16 [64, 1024, 1024], P('col', 'row')
- updated: bfloat16 [32, 12, 1024, 1024], P('col', None, 'row')
Inputs may be any that keep to these rules, and one draw needn't show every extreme that they name: Slot s of grid column c holds the tile at tile row slot_rows[c, s] and tile column 2 * c + slot_cols[c, s] of the trailing matrix, or nothing where slot_rows[c, s] is -1. Live slots come first in each column; the pairs of one column are distinct and lie on or below the diagonal (tile row at least tile column). Within one grid column, live slots whose tile rows a and a' have a // 2 == a' // 2 have a == a'. Every column holds at least one live slot, column 0 fills all 12 slots and column 16 holds exactly one. `slot_cols`: 0 in empty slots.
All inputs are finite; a program needn't handle non-finite values.
Results may differ from a plain program's by a relative error of at most 0.0019.
Values may be sent and summed in bfloat16 or wider, within the bound.
No kernel may reach another device: no remote copies, remote signals or barrier semaphores. Data moves between devices by JAX's collectives and lax.ppermute only.
A program may use at most 128 MiB of HBM per device.

v0:
```python
import jax
import jax.numpy as jnp
from jax import lax
from jax.sharding import PartitionSpec as P


def slot_product(slices, left_ids, source_tiles, col_ids, position):
    left_slice = lax.dynamic_index_in_dim(slices, left_ids[position], 0, keepdims=False)
    right_tile = lax.dynamic_index_in_dim(source_tiles, col_ids[position], 0, keepdims=False)
    return lax.dot_general(
        left_slice, right_tile, (((1,), (1,)), ((), ())), preferred_element_type=jnp.float32
    )


def subtract_slot(buffer, position, update):
    previous = lax.dynamic_index_in_dim(buffer, position, 0, keepdims=False).astype(jnp.float32)
    return lax.dynamic_update_index_in_dim(
        buffer, (previous - update).astype(jnp.bfloat16), position, 0
    )


def local(diag_block, panel, trailing, slot_rows, slot_cols):
    diag_full = lax.all_gather(diag_block, "row", axis=0, tiled=True)
    factor = jnp.linalg.cholesky(diag_full)
    tile_count, row_count, tile_width = panel.shape
    stacked = panel.astype(jnp.float32).reshape(tile_count * row_count, tile_width)
    solved = lax.linalg.triangular_solve(factor, stacked.T, left_side=True, lower=True)
    panel_factor = solved.T.reshape(tile_count, row_count, tile_width).astype(jnp.bfloat16)
    whole_tiles = lax.all_gather(panel_factor, "row", axis=1, tiled=True)
    column_index = lax.axis_index("col")
    own_rows = lax.dynamic_index_in_dim(slot_rows, column_index, 0, keepdims=False)
    own_cols = lax.dynamic_index_in_dim(slot_cols, column_index, 0, keepdims=False)
    own_count = jnp.sum((own_rows >= 0).astype(jnp.int32))
    slices = lax.all_gather(panel_factor, "col", axis=0, tiled=True)

    def own_step(position, buffer):
        return subtract_slot(
            buffer, position, slot_product(slices, own_rows, whole_tiles, own_cols, position)
        )

    buffer = lax.fori_loop(0, own_count, own_step, trailing[0])
    return (panel_factor, buffer[None])


def solution(mesh):
    return jax.shard_map(
        local,
        mesh=mesh,
        in_specs=(P("row", None), P("col", "row", None), P("col", None, "row", None), P(), P()),
        out_specs=(P("col", "row", None), P("col", None, "row", None)),
        check_vma=False,
    )
```

profile of v0, /device:TPU:1, one launch (start us, length us, event | category | flops | bytes accessed | tf_op | source)
XLA Modules:
  0.0 681.8 jit_solution(6531067428901336610)
XLA Ops:
  9.6 43.7 %all-gather.4.cloned.1.call-done = f32[1024,1024]{0,1:T(8,128)} async-done(((f32[128,1024]{0,1:T(8,128)}), f32[1024,1024]{0,1:T(8,128)}) %all-gather.4.cloned.1.call-update) | async-done | bytes 4194320 | tf_op jit(solution)/shard_map/all_gather | solution.py:23
  53.3 5.3 copy.18
  58.7 4.4 fusion.18
  65.0 11.7 %cholesky.223 = f32[128,128]{1,0:T(8,128)S(1)} custom-call(f32[128,128]{1,0:T(8,128)S(1)} %cholesky.580), custom_call_target="Cholesky" | custom-call | tf_op jit(solution)/shard_map/jit(cholesky)/cholesky | solution.py:24
  76.8 9.8 %custom-call.62 = f32[1,128,128]{1,2,0:T(8,128)S(1)} custom-call(f32[1,128,128]{2,1,0:T(8,128)S(1)} %get-tuple-element.117), custom_call_target="InvertDiagBlocksLowerTriangular" | custom-call | tf_op jit(solution)/shard_map/jit(cholesky)/cholesky | solution.py:24
  86.6 2.5 cholesky.255
  89.1 2.4 constant_dynamic-update-slice_fusion.24
  93.0 12.2 %cholesky.244 = f32[128,128]{1,0:T(8,128)S(1)} custom-call(f32[128,128]{1,0:T(8,128)S(1)} %cholesky.584), custom_call_target="Cholesky" | custom-call | tf_op jit(solution)/shard_map/jit(cholesky)/cholesky | solution.py:24
  105.8 9.8 %custom-call.63 = f32[1,128,128]{1,2,0:T(8,128)S(1)} custom-call(f32[1,128,128]{2,1,0:T(8,128)S(1)} %get-tuple-element.114), custom_call_target="InvertDiagBlocksLowerTriangular" | custom-call | tf_op jit(solution)/shard_map/jit(cholesky)/cholesky | solution.py:24
  119.0 11.7 %cholesky.468 = f32[128,128]{1,0:T(8,128)S(1)} custom-call(f32[128,128]{1,0:T(8,128)S(1)} %cholesky.589), custom_call_target="Cholesky" | custom-call | tf_op jit(solution)/shard_map/jit(cholesky)/cholesky | solution.py:24
  132.0 9.8 %custom-call.64 = f32[1,128,128]{1,2,0:T(8,128)S(1)} custom-call(f32[1,128,128]{2,1,0:T(8,128)S(1)} %get-tuple-element.111), custom_call_target="InvertDiagBlocksLowerTriangular" | custom-call | tf_op jit(solution)/shard_map/jit(cholesky)/cholesky | solution.py:24
  143.0 2.3 convolution_subtract_fusion.2
  145.3 11.8 %cholesky.487 = f32[128,128]{1,0:T(8,128)S(1)} custom-call(f32[128,128]{1,0:T(8,128)S(1)} %cholesky.594), custom_call_target="Cholesky" | custom-call | tf_op jit(solution)/shard_map/jit(cholesky)/cholesky | solution.py:24
  158.5 9.8 %custom-call.65 = f32[1,128,128]{1,2,0:T(8,128)S(1)} custom-call(f32[1,128,128]{2,1,0:T(8,128)S(1)} %get-tuple-element.108), custom_call_target="InvertDiagBlocksLowerTriangular" | custom-call | tf_op jit(solution)/shard_map/jit(cholesky)/cholesky | solution.py:24
  169.4 2.3 convolution_subtract_fusion.3
  171.7 11.7 %cholesky.506 = f32[128,128]{1,0:T(8,128)S(1)} custom-call(f32[128,128]{1,0:T(8,128)S(1)} %cholesky.599), custom_call_target="Cholesky" | custom-call | tf_op jit(solution)/shard_map/jit(cholesky)/cholesky | solution.py:24
  184.7 10.0 %custom-call.66 = f32[1,128,128]{1,2,0:T(8,128)S(1)} custom-call(f32[1,128,128]{2,1,0:T(8,128)S(1)} %get-tuple-element.105), custom_call_target="InvertDiagBlocksLowerTriangular" | custom-call | tf_op jit(solution)/shard_map/jit(cholesky)/cholesky | solution.py:24
  195.8 2.3 convolution_subtract_fusion.4
  198.1 11.7 %cholesky.526 = f32[128,128]{1,0:T(8,128)S(1)} custom-call(f32[128,128]{1,0:T(8,128)S(1)} %cholesky.604), custom_call_target="Cholesky" | custom-call | tf_op jit(solution)/shard_map/jit(cholesky)/cholesky | solution.py:24
  211.0 9.8 %custom-call.67 = f32[1,128,128]{1,2,0:T(8,128)S(1)} custom-call(f32[1,128,128]{2,1,0:T(8,128)S(1)} %get-tuple-element.102), custom_call_target="InvertDiagBlocksLowerTriangular" | custom-call | tf_op jit(solution)/shard_map/jit(cholesky)/cholesky | solution.py:24
  223.8 12.1 %cholesky.546 = f32[128,128]{1,0:T(8,128)S(1)} custom-call(f32[128,128]{1,0:T(8,128)S(1)} %cholesky.609), custom_call_target="Cholesky" | custom-call | tf_op jit(solution)/shard_map/jit(cholesky)/cholesky | solution.py:24
  237.2 9.8 %custom-call.68 = f32[1,128,128]{1,2,0:T(8,128)S(1)} custom-call(f32[1,128,128]{2,1,0:T(8,128)S(1)} %get-tuple-element.99), custom_call_target="InvertDiagBlocksLowerTriangular" | custom-call | tf_op jit(solution)/shard_map/jit(cholesky)/cholesky | solution.py:24
  249.7 11.7 %cholesky.564 = f32[128,128]{1,0:T(8,128)S(1)} custom-call(f32[128,128]{1,0:T(8,128)S(1)} %convolution_subtract_fusion.13), custom_call_target="Cholesky" | custom-call | tf_op jit(solution)/shard_map/jit(cholesky)/cholesky | solution.py:24
  268.3 4.8 select_select_fusion
  273.1 23.0 %while.12 = (s32[]{:T(128)}, f32[1024,1024]{1,0:T(8,128)}, s32[8,2]{0,1:T(2,128)S(1)}, f32[8,128,128]{2,1,0:T(8,128)S(1)}, s32[]{:T(128)}) while((s32[]{:T(128)}, f32[1024,1024]{1,0:T(8,128)}, s32[8,2]{0,1:T(2,128)S(1)}, f32[8,128,128]{2,1,0:T(8,128)S(1)}, s32[]{:T(128)}) %tuple.74), condition=%wide.while_cond, body=%wide.while_body.sunk | while | flops 2 | bytes 131189 | solution.py:27
  273.7 2.3 bitcast_dynamic-update-slice_fusion.2
  276.6 2.3 bitcast_dynamic-update-slice_fusion.2
  279.5 2.3 bitcast_dynamic-update-slice_fusion.2
  282.4 2.3 bitcast_dynamic-update-slice_fusion.2
  285.2 2.3 bitcast_dynamic-update-slice_fusion.2
  288.1 2.3 bitcast_dynamic-update-slice_fusion.2
  291.0 2.3 bitcast_dynamic-update-slice_fusion.2
  296.1 78.8 %custom-call.69 = f32[8,128,128]{1,2,0:T(8,128)S(1)} custom-call(f32[8,128,128]{2,1,0:T(8,128)S(1)} %get-tuple-element.48), custom_call_target="InvertDiagBlocksLowerTriangular" | custom-call | tf_op jit(solution)/shard_map/triangular_solve | solution.py:27
  398.6 34.2 %all-gather.8.cloned.1.call-done = bf16[2,1024,1024]{2,1,0:T(8,128)(2,1)} async-done(((bf16[2,128,1024]{2,1,0:T(8,128)(2,1)}), bf16[2,1024,1024]{2,1,0:T(8,128)(2,1)}) %all-gather.8.cloned.1.call-update) | async-done | bytes 4194320 | tf_op jit(solution)/shard_map/all_gather | solution.py:29
  432.8 142.9 %all-gather.6.cloned.1.call-done = bf16[64,128,1024]{2,1,0:T(8,128)(2,1)} async-done(((bf16[2,128,1024]{2,1,0:T(8,128)(2,1)}), bf16[64,128,1024]{2,1,0:T(8,128)(2,1)}) %all-gather.6.cloned.1.call-update) | async-done | bytes 16777232 | tf_op jit(solution)/shard_map/all_gather | solution.py:34
  575.8 97.6 %while.11 = (s32[]{:T(128)}, bf16[12,128,1024]{2,1,0:T(8,128)(2,1)S(1)}, s32[]{:T(128)}, s32[12]{0:T(128)S(1)}, bf16[64,128,1024]{2,1,0:T(8,128)(2,1)}, /*index=...) while((s32[]{:T(128)}, ...), condition=%wide.region_18.19_spmd, body=%wide.region_17.18_spmd.sunk | while | flops 268828672 | bytes 3408139 | solution.py:41
  581.3 2.5 fusion.100
  589.4 2.5 fusion.100
  597.5 2.5 fusion.100
  605.6 2.5 fusion.100
  613.6 2.5 fusion.100
  621.7 2.5 fusion.100
  629.8 2.5 fusion.100
  637.9 2.5 fusion.100
  646.0 2.5 fusion.100
  654.1 2.5 fusion.100
  662.1 2.5 fusion.100
  670.2 2.5 fusion.100
  (140 shorter events, 74.0 us)
Async XLA Ops:
  7.2 1.0 copy-start.4
  7.2 2.1 copy-start.5
  7.2 46.1 %all-gather.4.cloned.1.call-start = ((), (), s32[]{:S(2)}) async-start(), calls=%async_computation | async-start | bytes 4718592 | tf_op jit(solution)/shard_map/all_gather | solution.py:23
  9.2 423.6 %all-gather.8.cloned.1.call-start = ((), (), s32[]{:S(2)}) async-start(), calls=%async_computation.2 | async-start | bytes 4718592 | tf_op jit(solution)/shard_map/all_gather | solution.py:29
  9.6 372.6 %copy-start.3 = (f32[1024,256]{1,0:T(8,128)}, f32[1024,256]{1,0:T(8,128)S(1)}, u32[]{:S(2)}) copy-start(f32[1024,256]{1,0:T(8,128)S(1)} %bitcast_convert_fusion) | copy-start | bytes 3145732
  63.1 1.9 copy-start
  374.9 9.7 %copy-start.6 = (f32[8,128,128]{1,2,0:T(8,128)}, f32[8,128,128]{1,2,0:T(8,128)S(1)}, u32[]{:S(2)}) copy-start(f32[8,128,128]{1,2,0:T(8,128)S(1)} %custom-call.69) | copy-start | bytes 1572868
  384.7 13.1 %copy-start.7 = (s32[32,12]{0,1:T(8,128)S(1)}, s32[32,12]{0,1:T(8,128)}, u32[]{:S(2)}) copy-start(s32[32,12]{0,1:T(8,128)} %param.11) | copy-start | bytes 4612
  384.7 13.1 %copy-start.8 = (s32[32,12]{0,1:T(8,128)S(1)}, s32[32,12]{0,1:T(8,128)}, u32[]{:S(2)}) copy-start(s32[32,12]{0,1:T(8,128)} %param.10) | copy-start | bytes 4612
  384.7 191.1 %copy-start.2 = (bf16[1,12,128,1024]{3,2,1,0:T(8,128)(2,1)S(1)}, bf16[1,12,128,1024]{3,2,1,0:T(8,128)(2,1)}, u32[]{:S(2)}) copy-start(bf16[1,12,128,1024]{3,2,1,0:T(8,128)(2,1)} %param.9) | copy-start | bytes 9437188
  397.0 178.7 %all-gather.6.cloned.1.call-start = ((), (), s32[]{:S(2)}) async-start(), calls=%async_computation.1 | async-start | bytes 17301504 | tf_op jit(solution)/shard_map/all_gather | solution.py:34
  673.4 1.7 copy-start.1
Sparse Core Ops, SparseCore 0:
  10.4 42.8 all-gather.3
  397.1 35.6 all-gather.7
  436.0 139.6 all-gather.5
where the time goes:
time: 693 us; the launch traced here: 682 us
  other arithmetic  261 us (38%)
  waiting for transfers between devices  222 us (32%)
  matrix products  73.2 us (11%)
  local copies, waits for them, and re-layouts  53.5 us (8%)
  loops' own time  52.9 us (8%)
  between operations  19.3 us (3%)
    another operation x30, other arithmetic, local(): factor = jnp.linalg.cholesky(diag_full)  173 us
    all_gather x1, waiting for transfers between devices, local(): slices = lax.all_gather(panel_factor, 'col', axis=0, tiled=True)  143 us
    another operation x3, other arithmetic, local(): lax.linalg.triangular_solve(factor, stacked.T, left_side=True, lower=True)  83.6 us
    another operation x1, loops' own time, local(): buffer = lax.fori_loop(0, own_count, own_step, trailing[0])  52.7 us
    all_gather x1, waiting for transfers between devices, local(): diag_full = lax.all_gather(diag_block, 'row', axis=0, tiled=True)  43.7 us
    all_gather x1, waiting for transfers between devices, local(): whole_tiles = lax.all_gather(panel_factor, 'row', axis=1, tiled=True)  34.2 us
    dot_general x12, matrix products, slot_product(): lax.dot_general(left_slice, right_tile, (((1,), (1,)), ((), ())), preferr...  30.3 us
    another operation x14, matrix products, local(): factor = jnp.linalg.cholesky(diag_full)  23.1 us
  transfers between devices with their start and end apart: 3, of which 3 were waited for; matrix products, arithmetic and copies ran while one was open for 0% of the time, Pallas kernels for 0%

commit v1 on v0

--- a/solution.py
+++ b/solution.py
@@ -26,7 +26,12 @@
     stacked = panel.astype(jnp.float32).reshape(tile_count * row_count, tile_width)
     solved = lax.linalg.triangular_solve(factor, stacked.T, left_side=True, lower=True)
     panel_factor = solved.T.reshape(tile_count, row_count, tile_width).astype(jnp.bfloat16)
-    whole_tiles = lax.all_gather(panel_factor, "row", axis=1, tiled=True)
+    ring = [panel_factor]
+    for hop in range(7):
+        ring.append(lax.ppermute(ring[-1], "row", [(dev, (dev + 1) % 8) for dev in range(8)]))
+    whole_tiles = jnp.roll(
+        jnp.concatenate(ring[::-1], axis=1), (lax.axis_index("row") + 1) * ring[0].shape[1], axis=1
+    )
     column_index = lax.axis_index("col")
     own_rows = lax.dynamic_index_in_dim(slot_rows, column_index, 0, keepdims=False)
     own_cols = lax.dynamic_index_in_dim(slot_cols, column_index, 0, keepdims=False)

time: 693 us -> 647 us (0.934)
  waiting for transfers between devices: 222 us -> 161 us
  starting transfers between devices: 0.12 us -> 15.3 us
  matrix products: 73.2 us -> 65.5 us
    all_gather x1, waiting for transfers between devices: 143 us -> 72.3 us  [local(): slices = lax.all_gather(panel_factor, 'col', axis=0, tiled=True)]
    ppermute x0 -> x7, waiting for transfers between devices: none -> 45 us  [local(): lax.ppermute(ring[-1], 'row', [(dev, (dev + 1) % 8) for dev in range(8)])]
    all_gather x1 -> x0, waiting for transfers between devices: 34.2 us -> none  [local(): whole_tiles = lax.all_gather(panel_factor, 'row', axis=1, tiled=True)]
    ppermute x0 -> x7, starting transfers between devices: none -> 15.2 us  [local(): lax.ppermute(ring[-1], 'row', [(dev, (dev + 1) % 8) for dev in range(8)])]
    another operation x15, matrix products: 19.7 us -> 12 us  [local(): lax.linalg.triangular_solve(factor, stacked.T, left_side=True, lower=True)]
  transfers between devices with their start and end apart: 3 -> 9, of which waited for: 3 -> 9; matrix products, arithmetic and copies ran while one was open for 0% -> 1% of each run, Pallas kernels for 0% -> 0%
where the time goes in v1:
time: 647 us; the launch traced here: 635 us
  other arithmetic  261 us (40%)
  waiting for transfers between devices  161 us (25%)
  matrix products  65.5 us (10%)
  local copies, waits for them, and re-layouts  59.8 us (9%)
  loops' own time  52.9 us (8%)
  between operations  19.6 us (3%)
  starting transfers between devices  15.3 us (2%)
    another operation x30, other arithmetic, local(): factor = jnp.linalg.cholesky(diag_full)  172 us
    another operation x3, other arithmetic, local(): lax.linalg.triangular_solve(factor, stacked.T, left_side=True, lower=True)  83.6 us
    all_gather x1, waiting for transfers between devices, local(): slices = lax.all_gather(panel_factor, 'col', axis=0, tiled=True)  72.3 us
    another operation x1, loops' own time, local(): buffer = lax.fori_loop(0, own_count, own_step, trailing[0])  52.7 us
    ppermute x7, waiting for transfers between devices, local(): lax.ppermute(ring[-1], 'row', [(dev, (dev + 1) % 8) for dev in range(8)])  45 us
    all_gather x1, waiting for transfers between devices, local(): diag_full = lax.all_gather(diag_block, 'row', axis=0, tiled=True)  43.7 us
    dot_general x12, matrix products, slot_product(): lax.dot_general(left_slice, right_tile, (((1,), (1,)), ((), ())), preferr...  30.3 us
    another operation x14, matrix products, local(): factor = jnp.linalg.cholesky(diag_full)  23.1 us
  transfers between devices with their start and end apart: 9, of which 9 were waited for; matrix products, arithmetic and copies ran while one was open for 1% of the time, Pallas kernels for 0%

profile of v1, /device:TPU:1, one launch (start us, length us, event | category | flops | bytes accessed | tf_op | source)
XLA Modules:
  0.0 635.4 jit_solution(8266441189054497562)
XLA Ops:
  9.6 43.7 %all-gather.3.cloned.1.call-done = f32[1024,1024]{0,1:T(8,128)} async-done(((f32[128,1024]{0,1:T(8,128)}), f32[1024,1024]{0,1:T(8,128)}) %all-gather.3.cloned.1.call-update) | async-done | bytes 4194320 | tf_op jit(solution)/shard_map/all_gather | solution.py:23
  53.3 5.3 copy.22
  58.7 4.4 fusion.18
  65.0 11.7 %cholesky.223 = f32[128,128]{1,0:T(8,128)S(1)} custom-call(f32[128,128]{1,0:T(8,128)S(1)} %cholesky.580), custom_call_target="Cholesky" | custom-call | tf_op jit(solution)/shard_map/jit(cholesky)/cholesky | solution.py:24
  76.8 9.8 %custom-call.62 = f32[1,128,128]{1,2,0:T(8,128)S(1)} custom-call(f32[1,128,128]{2,1,0:T(8,128)S(1)} %get-tuple-element.117), custom_call_target="InvertDiagBlocksLowerTriangular" | custom-call | tf_op jit(solution)/shard_map/jit(cholesky)/cholesky | solution.py:24
  86.6 2.5 cholesky.255
  93.0 12.2 %cholesky.244 = f32[128,128]{1,0:T(8,128)S(1)} custom-call(f32[128,128]{1,0:T(8,128)S(1)} %cholesky.584), custom_call_target="Cholesky" | custom-call | tf_op jit(solution)/shard_map/jit(cholesky)/cholesky | solution.py:24
  105.8 9.8 %custom-call.63 = f32[1,128,128]{1,2,0:T(8,128)S(1)} custom-call(f32[1,128,128]{2,1,0:T(8,128)S(1)} %get-tuple-element.114), custom_call_target="InvertDiagBlocksLowerTriangular" | custom-call | tf_op jit(solution)/shard_map/jit(cholesky)/cholesky | solution.py:24
  119.0 11.7 %cholesky.468 = f32[128,128]{1,0:T(8,128)S(1)} custom-call(f32[128,128]{1,0:T(8,128)S(1)} %cholesky.589), custom_call_target="Cholesky" | custom-call | tf_op jit(solution)/shard_map/jit(cholesky)/cholesky | solution.py:24
  132.0 9.8 %custom-call.64 = f32[1,128,128]{1,2,0:T(8,128)S(1)} custom-call(f32[1,128,128]{2,1,0:T(8,128)S(1)} %get-tuple-element.111), custom_call_target="InvertDiagBlocksLowerTriangular" | custom-call | tf_op jit(solution)/shard_map/jit(cholesky)/cholesky | solution.py:24
  145.4 11.8 %cholesky.487 = f32[128,128]{1,0:T(8,128)S(1)} custom-call(f32[128,128]{1,0:T(8,128)S(1)} %cholesky.594), custom_call_target="Cholesky" | custom-call | tf_op jit(solution)/shard_map/jit(cholesky)/cholesky | solution.py:24
  158.5 9.8 %custom-call.65 = f32[1,128,128]{1,2,0:T(8,128)S(1)} custom-call(f32[1,128,128]{2,1,0:T(8,128)S(1)} %get-tuple-element.108), custom_call_target="InvertDiagBlocksLowerTriangular" | custom-call | tf_op jit(solution)/shard_map/jit(cholesky)/cholesky | solution.py:24
  171.8 11.7 %cholesky.506 = f32[128,128]{1,0:T(8,128)S(1)} custom-call(f32[128,128]{1,0:T(8,128)S(1)} %cholesky.599), custom_call_target="Cholesky" | custom-call | tf_op jit(solution)/shard_map/jit(cholesky)/cholesky | solution.py:24
  184.8 10.0 %custom-call.66 = f32[1,128,128]{1,2,0:T(8,128)S(1)} custom-call(f32[1,128,128]{2,1,0:T(8,128)S(1)} %get-tuple-element.105), custom_call_target="InvertDiagBlocksLowerTriangular" | custom-call | tf_op jit(solution)/shard_map/jit(cholesky)/cholesky | solution.py:24
  198.1 11.7 %cholesky.526 = f32[128,128]{1,0:T(8,128)S(1)} custom-call(f32[128,128]{1,0:T(8,128)S(1)} %cholesky.604), custom_call_target="Cholesky" | custom-call | tf_op jit(solution)/shard_map/jit(cholesky)/cholesky | solution.py:24
  211.1 9.8 %custom-call.67 = f32[1,128,128]{1,2,0:T(8,128)S(1)} custom-call(f32[1,128,128]{2,1,0:T(8,128)S(1)} %get-tuple-element.102), custom_call_target="InvertDiagBlocksLowerTriangular" | custom-call | tf_op jit(solution)/shard_map/jit(cholesky)/cholesky | solution.py:24
  223.9 12.1 %cholesky.546 = f32[128,128]{1,0:T(8,128)S(1)} custom-call(f32[128,128]{1,0:T(8,128)S(1)} %cholesky.609), custom_call_target="Cholesky" | custom-call | tf_op jit(solution)/shard_map/jit(cholesky)/cholesky | solution.py:24
  237.2 9.8 %custom-call.68 = f32[1,128,128]{1,2,0:T(8,128)S(1)} custom-call(f32[1,128,128]{2,1,0:T(8,128)S(1)} %get-tuple-element.99), custom_call_target="InvertDiagBlocksLowerTriangular" | custom-call | tf_op jit(solution)/shard_map/jit(cholesky)/cholesky | solution.py:24
  249.6 11.7 %cholesky.564 = f32[128,128]{1,0:T(8,128)S(1)} custom-call(f32[128,128]{1,0:T(8,128)S(1)} %convolution_subtract_fusion.13), custom_call_target="Cholesky" | custom-call | tf_op jit(solution)/shard_map/jit(cholesky)/cholesky | solution.py:24
  268.2 4.8 select_select_fusion
  273.0 23.0 %while.12 = (s32[]{:T(128)}, f32[1024,1024]{1,0:T(8,128)}, s32[8,2]{0,1:T(2,128)S(1)}, f32[8,128,128]{2,1,0:T(8,128)S(1)}, s32[]{:T(128)}) while((s32[]{:T(128)}, f32[1024,1024]{1,0:T(8,128)}, s32[8,2]{0,1:T(2,128)S(1)}, f32[8,128,128]{2,1,0:T(8,128)S(1)}, s32[]{:T(128)}) %tuple.73), condition=%wide.while_cond, body=%wide.while_body.sunk | while | flops 2 | bytes 131181 | solution.py:27
  296.0 78.8 %custom-call.69 = f32[8,128,128]{1,2,0:T(8,128)S(1)} custom-call(f32[8,128,128]{2,1,0:T(8,128)S(1)} %get-tuple-element.48), custom_call_target="InvertDiagBlocksLowerTriangular" | custom-call | tf_op jit(solution)/shard_map/triangular_solve | solution.py:27
  389.2 6.4 %collective-permute-done = bf16[2,128,1024]{2,1,0:T(8,128)(2,1)S(1)} collective-permute-done((bf16[2,128,1024]{2,1,0:T(8,128)(2,1)}, bf16[2,128,1024]{2,1,0:T(8,128)(2,1)S(1)}, u32[]{:S(2)}, u32[]{:S(2)}) %collective-permute-start) | collective-permute-done | bytes 524320 | tf_op jit(solution)/shard_map/ppermute | solution.py:31
  398.0 6.1 collective-permute-done.1
  404.1 2.5 collective-permute-start.2
  406.6 6.1 collective-permute-done.2
  412.7 2.5 collective-permute-start.3
  415.2 6.1 collective-permute-done.3
  421.3 2.5 collective-permute-start.4
  423.8 6.1 collective-permute-done.4
  429.9 2.5 collective-permute-start.5
  432.4 6.8 %collective-permute-done.5 = bf16[2,128,1024]{2,1,0:T(8,128)(2,1)} collective-permute-done((bf16[2,128,1024]{2,1,0:T(8,128)(2,1)S(1)}, bf16[2,128,1024]{2,1,0:T(8,128)(2,1)}, u32[]{:S(2)}, u32[]{:S(2)}) %collective-permute-start.5) | collective-permute-done | bytes 524320 | tf_op jit(solution)/shard_map/ppermute | solution.py:31
  442.2 7.2 %collective-permute-done.6 = bf16[2,128,1024]{2,1,0:T(8,128)(2,1)} collective-permute-done((bf16[2,128,1024]{2,1,0:T(8,128)(2,1)}, bf16[2,128,1024]{2,1,0:T(8,128)(2,1)}, u32[]{:S(2)}, u32[]{:S(2)}) %collective-permute-start.6) | collective-permute-done | bytes 524320 | tf_op jit(solution)/shard_map/ppermute | solution.py:31
  454.3 2.4 constant_dynamic-slice_fusion.2
  456.7 72.3 %all-gather.5.cloned.1.call-done = bf16[64,128,1024]{2,1,0:T(8,128)(2,1)} async-done(((bf16[2,128,1024]{2,1,0:T(8,128)(2,1)}), bf16[64,128,1024]{2,1,0:T(8,128)(2,1)}) %all-gather.5.cloned.1.call-update) | async-done | bytes 16777232 | tf_op jit(solution)/shard_map/all_gather | solution.py:39
  529.0 97.6 %while.11 = (s32[]{:T(128)}, bf16[12,128,1024]{2,1,0:T(8,128)(2,1)S(1)}, s32[]{:T(128)}, s32[12]{0:T(128)S(1)}, bf16[64,128,1024]{2,1,0:T(8,128)(2,1)}, /*index=...) while((s32[]{:T(128)}, ...), condition=%wide.region_18.19_spmd, body=%wide.region_17.18_spmd.sunk | while | flops 268828672 | bytes 3408131 | solution.py:46
  534.6 2.5 fusion.100
  542.7 2.5 fusion.100
  550.8 2.5 fusion.100
  558.8 2.5 fusion.100
  566.9 2.5 fusion.100
  575.0 2.5 fusion.100
  583.1 2.5 fusion.100
  591.2 2.5 fusion.100
  599.3 2.5 fusion.100
  607.3 2.5 fusion.100
  615.4 2.5 fusion.100
  623.5 2.5 fusion.100
  (167 shorter events, 99.9 us)
Async XLA Ops:
  7.2 434.0 %copy-start = (s32[32,12]{0,1:T(8,128)S(1)}, s32[32,12]{0,1:T(8,128)}, u32[]{:S(2)}) copy-start(s32[32,12]{0,1:T(8,128)} %param.10) | copy-start | bytes 4612
  7.2 1.0 copy-start.5
  7.2 2.1 copy-start.6
  7.2 46.1 %all-gather.3.cloned.1.call-start = ((), (), s32[]{:S(2)}) async-start(), calls=%async_computation | async-start | bytes 4718592 | tf_op jit(solution)/shard_map/all_gather | solution.py:23
  9.2 519.8 %all-gather.5.cloned.1.call-start = ((), (), s32[]{:S(2)}) async-start(), calls=%async_computation.1 | async-start | bytes 17301504 | tf_op jit(solution)/shard_map/all_gather | solution.py:39
  63.1 1.9 copy-start.1
  381.4 59.9 %copy-start.7 = (s32[32,12]{0,1:T(8,128)S(1)}, s32[32,12]{0,1:T(8,128)}, u32[]{:S(2)}) copy-start(s32[32,12]{0,1:T(8,128)} %param.11) | copy-start | bytes 4612
  388.1 63.7 %copy-start.2 = (bf16[256,1024]{1,0:T(8,128)(2,1)S(1)}, bf16[256,1024]{1,0:T(8,128)(2,1)}, u32[]{:S(2)}) copy-start(bf16[256,1024]{1,0:T(8,128)(2,1)} %copy.30) | copy-start | bytes 1572868
  388.1 7.5 %collective-permute-start = (bf16[2,128,1024]{2,1,0:T(8,128)(2,1)}, bf16[2,128,1024]{2,1,0:T(8,128)(2,1)S(1)}, u32[]{:S(2)}, u32[]{:S(2)}) collective-permute-start(bf16[2,128,1024]{2,1,0:T(8,128)(2,1)} %bitcast.144), channel_id=1, source_target_pairs={{0,32},{32,64},{64,96},{96,128},{128,160},{160,192},{192,224},{224... | collective-permute-start | bytes 1572872 | tf_op jit(solution)/shard_map/ppermute | solution.py:31
  395.6 8.5 %collective-permute-start.1 = (bf16[2,128,1024]{2,1,0:T(8,128)(2,1)S(1)}, bf16[2,128,1024]{2,1,0:T(8,128)(2,1)S(1)}, u32[]{:S(2)}, u32[]{:S(2)}) collective-permute-start(bf16[2,128,1024]{2,1,0:T(8,128)(2,1)S(1)} %collective-permute-done), channel_id=1, source_target_pairs={{0,32},{32,64},{64,96},{96,128},{128,160},{160,192},{192,224},{224... | collective-permute-start | bytes 1572872 | tf_op jit(solution)/shard_map/ppermute | solution.py:31
  404.1 8.6 %collective-permute-start.2 = (bf16[2,128,1024]{2,1,0:T(8,128)(2,1)S(1)}, bf16[2,128,1024]{2,1,0:T(8,128)(2,1)S(1)}, u32[]{:S(2)}, u32[]{:S(2)}) collective-permute-start(bf16[2,128,1024]{2,1,0:T(8,128)(2,1)S(1)} %collective-permute-done.1), channel_id=1, source_target_pairs={{0,32},{32,64},{64,96},{96,128},{128,160},{160,192},{192,224},{224... | collective-permute-start | bytes 1572872 | tf_op jit(solution)/shard_map/ppermute | solution.py:31
  412.7 8.6 %collective-permute-start.3 = (bf16[2,128,1024]{2,1,0:T(8,128)(2,1)S(1)}, bf16[2,128,1024]{2,1,0:T(8,128)(2,1)S(1)}, u32[]{:S(2)}, u32[]{:S(2)}) collective-permute-start(bf16[2,128,1024]{2,1,0:T(8,128)(2,1)S(1)} %collective-permute-done.2), channel_id=1, source_target_pairs={{0,32},{32,64},{64,96},{96,128},{128,160},{160,192},{192,224},{224... | collective-permute-start | bytes 1572872 | tf_op jit(solution)/shard_map/ppermute | solution.py:31
  421.3 8.6 %collective-permute-start.4 = (bf16[2,128,1024]{2,1,0:T(8,128)(2,1)S(1)}, bf16[2,128,1024]{2,1,0:T(8,128)(2,1)S(1)}, u32[]{:S(2)}, u32[]{:S(2)}) collective-permute-start(bf16[2,128,1024]{2,1,0:T(8,128)(2,1)S(1)} %collective-permute-done.3), channel_id=1, source_target_pairs={{0,32},{32,64},{64,96},{96,128},{128,160},{160,192},{192,224},{224... | collective-permute-start | bytes 1572872 | tf_op jit(solution)/shard_map/ppermute | solution.py:31
  429.9 9.3 %collective-permute-start.5 = (bf16[2,128,1024]{2,1,0:T(8,128)(2,1)S(1)}, bf16[2,128,1024]{2,1,0:T(8,128)(2,1)}, u32[]{:S(2)}, u32[]{:S(2)}) collective-permute-start(bf16[2,128,1024]{2,1,0:T(8,128)(2,1)S(1)} %collective-permute-done.4), channel_id=1, source_target_pairs={{0,32},{32,64},{64,96},{96,128},{128,160},{160,192},{192,224},{224... | collective-permute-start | bytes 1572872 | tf_op jit(solution)/shard_map/ppermute | solution.py:31
  439.3 10.1 %collective-permute-start.6 = (bf16[2,128,1024]{2,1,0:T(8,128)(2,1)}, bf16[2,128,1024]{2,1,0:T(8,128)(2,1)}, u32[]{:S(2)}, u32[]{:S(2)}) collective-permute-start(bf16[2,128,1024]{2,1,0:T(8,128)(2,1)} %collective-permute-done.5), channel_id=1, source_target_pairs={{0,32},{32,64},{64,96},{96,128},{128,160},{160,192},{192,224},{224... | collective-permute-start | bytes 1572872 | tf_op jit(solution)/shard_map/ppermute | solution.py:31
  454.3 74.7 %copy-start.4 = (bf16[1,12,128,1024]{3,2,1,0:T(8,128)(2,1)S(1)}, bf16[1,12,128,1024]{3,2,1,0:T(8,128)(2,1)}, u32[]{:S(2)}) copy-start(bf16[1,12,128,1024]{3,2,1,0:T(8,128)(2,1)} %param.9) | copy-start | bytes 9437188
  626.7 1.7 copy-start.3
Sparse Core Ops, SparseCore 0:
  10.4 42.8 all-gather.2
  388.3 140.7 all-gather.4
